TPU v7x, 256 devices: a whole 4x4x8 slice. The times are simulated.
256 devices in a mesh: blk: 64 (over z_lo, x, y), grp: 4 (over z_hi, core).
Axes of the slice: x: 4, y: 4, z: 8 (z_hi: 2, z_lo: 4; z = z_hi * 4 + z_lo), core: 2. Of those that a mesh axis runs over, the one named last changes fastest.
Arguments:
- source_embed: bfloat16 [131072, 768], P(('blk', 'grp')), may hold values from -60 to 60
- target_embed: bfloat16 [8192, 768], P('blk'), may hold values from -18 to 18
- target_init: float32 [8192], P('blk'), may hold values from -6 to 6
- source_logw: float32 [131072], P(('blk', 'grp')), may hold values from -2 to 2
- target_logw: float32 [8192], P('blk'), may hold values from -2 to 2
Outputs:
- row_pot: float32 [131072], P(('blk', 'grp'))
- column_pot: float32 [8192], P('blk')
All inputs are finite; a program needn't handle non-finite values.
Results may differ from a plain program's by a relative error of at most 0.0003.
Values may be sent and summed in bfloat16 or wider, within the bound.
A program may use at most 128 MiB of HBM per device.

v0:
```python
import math
import jax
import jax.numpy as jnp
from jax import lax
from jax.sharding import PartitionSpec as P

D = 768
ITERS = 2
epsilon = 0.1
inverse_eps = 10.0


def row_update(cost_matrix, column_pot, row_logw):
    scores = (column_pot[None, :] - cost_matrix) * inverse_eps
    row_top = jnp.max(scores, axis=1)
    row_sum = jnp.sum(jnp.exp(scores - row_top[:, None]), axis=1)
    return epsilon * row_logw - epsilon * (row_top + jnp.log(row_sum))


def shards(source_embed, target_embed, target_init, source_logw, target_logw):
    factor = -1.0 / math.sqrt(D)
    init_full, logw_full = (
        lax.all_gather(target_init, "blk", axis=0, tiled=True),
        lax.all_gather(target_logw, "blk", axis=0, tiled=True),
    )
    block_index = lax.axis_index("blk")
    rows_target = target_embed.shape[0]
    cost_matrix = (
        lax.dot_general(
            source_embed,
            lax.all_gather(target_embed, "blk", axis=0, tiled=True),
            (((1,), (1,)), ((), ())),
            preferred_element_type=jnp.float32,
        )
        * factor
    )
    column_pot = init_full
    row_pot = jnp.zeros(source_logw.shape, jnp.float32)
    for iteration in range(ITERS):
        row_pot = row_update(cost_matrix, column_pot, source_logw)
        scores = (row_pot[:, None] - cost_matrix) * inverse_eps
        col_top = jnp.max(scores, axis=0)
        col_peak = lax.pmax(col_top.astype(jnp.bfloat16), ("blk", "grp")).astype(col_top.dtype)
        col_total = lax.psum(jnp.sum(jnp.exp(scores - col_peak[None, :]), axis=0), ("blk", "grp"))
        column_pot = epsilon * logw_full - epsilon * (col_peak + jnp.log(col_total))
    return (
        row_pot,
        lax.dynamic_slice_in_dim(column_pot, block_index * rows_target, rows_target, 0),
    )


def solution(mesh):
    in_specs = (P(("blk", "grp"), None), P("blk", None), P("blk"), P(("blk", "grp")), P("blk"))
    out_specs = (P(("blk", "grp")), P("blk"))
    return jax.shard_map(shards, mesh=mesh, in_specs=in_specs, out_specs=out_specs, check_vma=False)
```

profile of v0, /device:TPU:1, one launch (start us, length us, event | category | flops | bytes accessed | tf_op | source)
XLA Modules:
  0.0 764.0 jit_solution(6717112200024269160)
XLA Ops:
  7.2 0.0 copy-start
  7.2 0.0 all-gather.4.cloned.1.call-start
  7.2 0.7 all-gather.4.cloned.1.call-update
  7.9 164.8 %all-gather.1 = f32[64,1,128]{2,1,0:T(1,128)S(1)} all-gather(f32[1,1,128]{2,1,0:T(1,128)} %bitcast.10), channel_id=1, replica_groups=mesh['blk'=64,'grp'=4] {'blk'}, dimensions={0}, use_global_device_ids=true | all-gather | bytes 33280 | tf_op jit(solution)/shard_map/all_gather | solution.py:23
  172.7 155.8 %all-gather = f32[64,1,128]{2,1,0:T(1,128)S(1)} all-gather(f32[1,1,128]{2,1,0:T(1,128)} %bitcast.11), channel_id=1, replica_groups=mesh['blk'=64,'grp'=4] {'blk'}, dimensions={0}, use_global_device_ids=true | all-gather | bytes 33280 | tf_op jit(solution)/shard_map/all_gather | solution.py:24
  328.5 12.5 %all-gather.4.cloned.1.call-done = bf16[8192,768]{1,0:T(8,128)(2,1)} async-done(((bf16[128,768]{1,0:T(8,128)(2,1)}), bf16[8192,768]{1,0:T(8,128)(2,1)}) %all-gather.4.cloned.1.call-update) | async-done | bytes 12582928 | tf_op jit(solution)/shard_map/all_gather | solution.py:31
  341.0 0.0 copy-done
  341.0 14.9 %fusion = (f32[512]{0:T(512)S(1)}, f32[512,8192]{1,0:T(8,128)}) fusion(f32[8192]{0:T(1024)S(1)} %bitcast.8, bf16[512,768]{1,0:T(8,128)(2,1)S(1)} %copy-done, bf16[8192,768]{1,0:T(8,128)(2,1)} %all-gather.4.cloned.1.call-done), kind=kOutput, calls=%fused_computation.8 | convolution fusion | flops 6459227648 | bytes 30181376 | tf_op jit(solution)/shard_map/dot_general | solution.py:29
  355.9 0.0 copy-start.2
  355.9 9.3 %exponential_reduce_fusion.3 = f32[512]{0:T(512)S(1)} fusion(f32[512,8192]{1,0:T(8,128)} %get-tuple-element.3, f32[512]{0:T(512)S(1)} %get-tuple-element.2, f32[8192]{0:T(1024)S(1)} %bitcast.9), kind=kLoop, calls=%fused_computation.6 | loop fusion | flops 16776704 | bytes 16814080 | tf_op jit(solution)/shard_map/reduce_sum | solution.py:16
  365.3 0.0 copy-done.2
  365.3 8.4 %fusion.1 = bf16[8192]{0:T(1024)(128)(2,1)S(1)} fusion(f32[512,8192]{1,0:T(8,128)} %get-tuple-element.3, f32[512]{0:T(512)S(1)} %multiply_subtract_fusion.2), kind=kLoop, calls=%fused_computation.9 | loop fusion | flops 12574720 | bytes 16795648 | tf_op jit(solution)/shard_map/reduce_max | solution.py:42
  373.7 117.5 %pmax.14 = bf16[8192]{0:T(1024)(128)(2,1)S(1)} all-reduce(bf16[8192]{0:T(1024)(128)(2,1)S(1)} %fusion.1), channel_id=1, replica_groups=mesh['blk'=64,'grp'=4] {'blk','grp'}, use_global_device_ids=true, to_apply=%region_3.0 | all-reduce | flops 8192 | bytes 32768 | tf_op jit(solution)/shard_map/pmax | solution.py:43
  491.1 9.4 %exponential_reduce_fusion.2 = f32[8192]{0:T(1024)S(1)} fusion(f32[512,8192]{1,0:T(8,128)} %get-tuple-element.3, f32[8192]{0:T(1024)S(1)} %convert_element_type.13, f32[512]{0:T(512)S(1)} %multiply_subtract_fusion.2), kind=kLoop, calls=%fused_computation.4 | loop fusion | flops 16769024 | bytes 16844800 | tf_op jit(solution)/shard_map/reduce_sum | solution.py:44
  500.6 72.9 %psum.14 = f32[8192]{0:T(1024)S(1)} all-reduce(f32[8192]{0:T(1024)S(1)} %exponential_reduce_fusion.2), channel_id=1, replica_groups=mesh['blk'=64,'grp'=4] {'blk','grp'}, use_global_device_ids=true, to_apply=%region_5.0 | all-reduce | flops 8192 | bytes 65536 | tf_op jit(solution)/shard_map/psum | solution.py:44
  573.5 7.7 %fusion.2 = f32[512]{0:T(512)S(1)} fusion(f32[512,8192]{1,0:T(8,128)} %get-tuple-element.3, f32[8192]{0:T(1024)S(1)} %multiply_subtract_fusion), kind=kLoop, calls=%fused_computation.10 | loop fusion | flops 12582400 | bytes 16812032 | tf_op jit(solution)/shard_map/reduce_max | solution.py:15
  581.2 9.3 %exponential_reduce_fusion.1 = f32[512]{0:T(512)S(1)} fusion(f32[512,8192]{1,0:T(8,128)} %get-tuple-element.3, f32[512]{0:T(512)S(1)} %fusion.2, f32[8192]{0:T(1024)S(1)} %multiply_subtract_fusion), kind=kLoop, calls=%fused_computation.2 | loop fusion | flops 16776704 | bytes 16814080 | tf_op jit(solution)/shard_map/reduce_sum | solution.py:16
  590.6 0.0 copy-start.1
  590.6 8.4 %fusion.3 = bf16[8192]{0:T(1024)(128)(2,1)S(1)} fusion(f32[512,8192]{1,0:T(8,128)} %get-tuple-element.3, f32[512]{0:T(512)S(1)} %multiply_subtract_fusion.1), kind=kLoop, calls=%fused_computation.11 | loop fusion | flops 12574720 | bytes 16795648 | tf_op jit(solution)/shard_map/reduce_max | solution.py:42
  598.9 74.6 %pmax.15 = bf16[8192]{0:T(1024)(128)(2,1)S(1)} all-reduce(bf16[8192]{0:T(1024)(128)(2,1)S(1)} %fusion.3), channel_id=1, replica_groups=mesh['blk'=64,'grp'=4] {'blk','grp'}, use_global_device_ids=true, to_apply=%region_9.0 | all-reduce | flops 8192 | bytes 32768 | tf_op jit(solution)/shard_map/pmax | solution.py:43
  673.6 9.4 %exponential_reduce_fusion = f32[8192]{0:T(1024)S(1)} fusion(f32[512,8192]{1,0:T(8,128)} %get-tuple-element.3, f32[8192]{0:T(1024)S(1)} %convert_element_type.15, f32[512]{0:T(512)S(1)} %multiply_subtract_fusion.1), kind=kLoop, calls=%fused_computation | loop fusion | flops 16769024 | bytes 16844800 | tf_op jit(solution)/shard_map/reduce_sum | solution.py:44
  683.0 0.0 copy-done.1
  683.0 73.5 %psum.15 = f32[8192]{0:T(1024)S(1)} all-reduce(f32[8192]{0:T(1024)S(1)} %exponential_reduce_fusion), channel_id=1, replica_groups=mesh['blk'=64,'grp'=4] {'blk','grp'}, use_global_device_ids=true, to_apply=%region_11.0 | all-reduce | flops 8192 | bytes 65536 | tf_op jit(solution)/shard_map/psum | solution.py:44
  756.5 0.6 dynamic-slice_subtract_fusion
  (6 shorter events, 0.1 us)
Async XLA Ops:
  7.2 333.8 %copy-start = (bf16[512,768]{1,0:T(8,128)(2,1)S(1)}, bf16[512,768]{1,0:T(8,128)(2,1)}, u32[]{:S(2)}) copy-start(bf16[512,768]{1,0:T(8,128)(2,1)} %param.5) | copy-start | bytes 2359300
  7.2 333.8 %all-gather.4.cloned.1.call-start = ((), (), s32[]{:S(2)}) async-start(), calls=%async_computation | async-start | bytes 12779520 | tf_op jit(solution)/shard_map/all_gather | solution.py:31
  355.9 9.3 %copy-start.2 = (f32[512]{0:T(512)S(1)}, f32[512]{0:T(512)}, u32[]{:S(2)}) copy-start(f32[512]{0:T(512)} %param.8) | copy-start | bytes 6148
  590.6 92.5 %copy-start.1 = (f32[512]{0:T(512)}, f32[512]{0:T(512)S(1)}, u32[]{:S(2)}) copy-start(f32[512]{0:T(512)S(1)} %multiply_subtract_fusion.1) | copy-start | bytes 6148
Sparse Core Ops, SparseCore 0:
  9.8 331.1 all-gather.3
where the time goes:
time: 765 us; the launch traced here: 764 us
  blocking collectives  659 us (86%)
  other arithmetic  62.7 us (8%)
  matrix products  14.9 us (2%)
  between operations  14.1 us (2%)
  waiting for transfers between devices  13.2 us (2%)
    pmax x2, blocking collectives, shards(): lax.pmax(col_top.astype(jnp.bfloat16), ('blk', 'grp')).astype(col_top.dtype)  192 us
    all_gather x1, blocking collectives, shards(): lax.all_gather(target_init, 'blk', axis=0, tiled=True)  165 us
    all_gather x1, blocking collectives, shards(): lax.all_gather(target_logw, 'blk', axis=0, tiled=True)  156 us
    psum x2, blocking collectives, shards(): lax.psum(jnp.sum(jnp.exp(scores - col_peak[None, :]), axis=0), ('blk', 'g...  146 us
    reduce_sum x2, other arithmetic, shards(): jnp.sum(jnp.exp(scores - col_peak[None, :]), axis=0)  18.9 us
    reduce_sum x2, other arithmetic, row_update(): row_sum = jnp.sum(jnp.exp(scores - row_top[:, None]), axis=1)  18.7 us
    reduce_max x2, other arithmetic, shards(): col_top = jnp.max(scores, axis=0)  16.7 us
  transfers between devices with their start and end apart: 1, of which 1 were waited for; matrix products, arithmetic and copies ran while one was open for 0% of the time, Pallas kernels for 0%

commit v1 on v0

--- a/solution.py
+++ b/solution.py
@@ -21,7 +21,9 @@
     factor = -1.0 / math.sqrt(D)
     init_full, logw_full = (
         lax.all_gather(target_init, "blk", axis=0, tiled=True),
-        lax.all_gather(target_logw, "blk", axis=0, tiled=True),
+        jnp.concatenate(
+            lax.all_to_all(jnp.stack([target_logw] * lax.axis_size("blk")), "blk", 0, 0), axis=0
+        ),
     )
     block_index = lax.axis_index("blk")
     rows_target = target_embed.shape[0]

time: 765 us -> 765 us (level)
  blocking collectives: 659 us -> 502 us
  waiting for transfers between devices: 13.2 us -> 157 us
  starting transfers between devices: 0.04 us -> 12.6 us
    all_gather x1 -> x0, blocking collectives: 156 us -> none  [shards(): lax.all_gather(target_logw, 'blk', axis=0, tiled=True)]
    all_gather x1, waiting for transfers between devices: 12.5 us -> 156 us  [shards(): lax.all_gather(target_embed, 'blk', axis=0, tiled=True)]
    all_to_all x0 -> x1, starting transfers between devices: none -> 12.5 us  [shards(): lax.all_to_all(jnp.stack([target_logw] * lax.axis_size('blk')), 'blk', 0, 0)]
  transfers between devices with their start and end apart: 1 -> 2, of which waited for: 1 -> 1; matrix products, arithmetic and copies ran while one was open for 0% -> 0% of each run, Pallas kernels for 0% -> 0%
where the time goes in v1:
time: 765 us; the launch traced here: 764 us
  blocking collectives  502 us (66%)
  waiting for transfers between devices  157 us (21%)
  other arithmetic  62.5 us (8%)
  matrix products  14.9 us (2%)
  between operations  14.1 us (2%)
  starting transfers between devices  12.6 us (2%)
    pmax x2, blocking collectives, shards(): lax.pmax(col_top.astype(jnp.bfloat16), ('blk', 'grp')).astype(col_top.dtype)  192 us
    all_gather x1, blocking collectives, shards(): lax.all_gather(target_init, 'blk', axis=0, tiled=True)  163 us
    all_gather x1, waiting for transfers between devices, shards(): lax.all_gather(target_embed, 'blk', axis=0, tiled=True)  156 us
    psum x2, blocking collectives, shards(): lax.psum(jnp.sum(jnp.exp(scores - col_peak[None, :]), axis=0), ('blk', 'g...  146 us
    reduce_sum x2, other arithmetic, shards(): jnp.sum(jnp.exp(scores - col_peak[None, :]), axis=0)  18.9 us
    reduce_sum x2, other arithmetic, row_update(): row_sum = jnp.sum(jnp.exp(scores - row_top[:, None]), axis=1)  18.5 us
    reduce_max x2, other arithmetic, shards(): col_top = jnp.max(scores, axis=0)  16.7 us
  transfers between devices with their start and end apart: 2, of which 1 were waited for; matrix products, arithmetic and copies ran while one was open for 0% of the time, Pallas kernels for 0%

profile of v1, /device:TPU:1, one launch (start us, length us, event | category | flops | bytes accessed | tf_op | source)
XLA Modules:
  0.0 763.8 jit_solution(5612828132549494760)
XLA Ops:
  7.2 0.0 copy-start
  7.2 0.0 all-gather.3.cloned.1.call-start
  7.2 0.7 all-gather.3.cloned.1.call-update
  7.9 1.3 stack.2
  9.2 12.5 %all-to-all-start = ((f32[64,1,128]{2,1,0:T(1,128)}), f32[64,1,128]{2,1,0:T(1,128)S(1)}, u32[]{:S(2)}, u32[]{:S(2)}) async-start(f32[64,1,128]{2,1,0:T(1,128)} %stack.2), calls=%async_computation | async-start | bytes 65536 | tf_op jit(solution)/shard_map/all_to_all | solution.py:25
  21.7 163.2 %all-gather = f32[64,1,128]{2,1,0:T(1,128)S(1)} all-gather(f32[1,1,128]{2,1,0:T(1,128)} %bitcast.9), channel_id=1, replica_groups=mesh['blk'=64,'grp'=4] {'blk'}, dimensions={0}, use_global_device_ids=true | all-gather | bytes 33280 | tf_op jit(solution)/shard_map/all_gather | solution.py:23
  184.9 0.0 all-to-all-done
  185.0 156.0 %all-gather.3.cloned.1.call-done = bf16[8192,768]{1,0:T(8,128)(2,1)} async-done(((bf16[128,768]{1,0:T(8,128)(2,1)}), bf16[8192,768]{1,0:T(8,128)(2,1)}) %all-gather.3.cloned.1.call-update) | async-done | bytes 12582928 | tf_op jit(solution)/shard_map/all_gather | solution.py:33
  341.0 0.0 copy-done
  341.0 14.9 %fusion = (f32[512]{0:T(512)S(1)}, f32[512,8192]{1,0:T(8,128)}) fusion(f32[8192]{0:T(1024)S(1)} %bitcast.7, bf16[512,768]{1,0:T(8,128)(2,1)S(1)} %copy-done, bf16[8192,768]{1,0:T(8,128)(2,1)} %all-gather.3.cloned.1.call-done), kind=kOutput, calls=%fused_computation.8 | convolution fusion | flops 6459227648 | bytes 30181376 | tf_op jit(solution)/shard_map/dot_general | solution.py:31
  356.0 9.2 %exponential_reduce_fusion.3 = f32[512]{0:T(512)S(1)} fusion(f32[512,8192]{1,0:T(8,128)} %get-tuple-element.3, f32[512]{0:T(512)S(1)} %get-tuple-element.2, f32[8192]{0:T(1024)S(1)} %bitcast.8), kind=kLoop, calls=%fused_computation.6 | loop fusion | flops 16776704 | bytes 16814080 | tf_op jit(solution)/shard_map/reduce_sum | solution.py:16
  365.1 0.0 copy-done.2
  365.1 8.4 %fusion.1 = bf16[8192]{0:T(1024)(128)(2,1)S(1)} fusion(f32[512,8192]{1,0:T(8,128)} %get-tuple-element.3, f32[512]{0:T(512)S(1)} %multiply_subtract_fusion.2), kind=kLoop, calls=%fused_computation.9 | loop fusion | flops 12574720 | bytes 16795648 | tf_op jit(solution)/shard_map/reduce_max | solution.py:44
  373.5 118.4 %pmax.14 = bf16[8192]{0:T(1024)(128)(2,1)S(1)} all-reduce(bf16[8192]{0:T(1024)(128)(2,1)S(1)} %fusion.1), channel_id=1, replica_groups=mesh['blk'=64,'grp'=4] {'blk','grp'}, use_global_device_ids=true, to_apply=%region_3.0 | all-reduce | flops 8192 | bytes 32768 | tf_op jit(solution)/shard_map/pmax | solution.py:45
  491.9 9.4 %exponential_reduce_fusion.2 = f32[8192]{0:T(1024)S(1)} fusion(f32[512,8192]{1,0:T(8,128)} %get-tuple-element.3, f32[8192]{0:T(1024)S(1)} %convert_element_type.13, f32[512]{0:T(512)S(1)} %multiply_subtract_fusion.2), kind=kLoop, calls=%fused_computation.4 | loop fusion | flops 16769024 | bytes 16844800 | tf_op jit(solution)/shard_map/reduce_sum | solution.py:46
  501.4 72.7 %psum.14 = f32[8192]{0:T(1024)S(1)} all-reduce(f32[8192]{0:T(1024)S(1)} %exponential_reduce_fusion.2), channel_id=1, replica_groups=mesh['blk'=64,'grp'=4] {'blk','grp'}, use_global_device_ids=true, to_apply=%region_5.0 | all-reduce | flops 8192 | bytes 65536 | tf_op jit(solution)/shard_map/psum | solution.py:46
  574.1 7.7 %fusion.2 = f32[512]{0:T(512)S(1)} fusion(f32[512,8192]{1,0:T(8,128)} %get-tuple-element.3, f32[8192]{0:T(1024)S(1)} %multiply_subtract_fusion), kind=kLoop, calls=%fused_computation.10 | loop fusion | flops 12582400 | bytes 16812032 | tf_op jit(solution)/shard_map/reduce_max | solution.py:15
  581.9 9.3 %exponential_reduce_fusion.1 = f32[512]{0:T(512)S(1)} fusion(f32[512,8192]{1,0:T(8,128)} %get-tuple-element.3, f32[512]{0:T(512)S(1)} %fusion.2, f32[8192]{0:T(1024)S(1)} %multiply_subtract_fusion), kind=kLoop, calls=%fused_computation.2 | loop fusion | flops 16776704 | bytes 16814080 | tf_op jit(solution)/shard_map/reduce_sum | solution.py:16
  591.2 0.0 copy-start.1
  591.2 8.4 %fusion.3 = bf16[8192]{0:T(1024)(128)(2,1)S(1)} fusion(f32[512,8192]{1,0:T(8,128)} %get-tuple-element.3, f32[512]{0:T(512)S(1)} %multiply_subtract_fusion.1), kind=kLoop, calls=%fused_computation.11 | loop fusion | flops 12574720 | bytes 16795648 | tf_op jit(solution)/shard_map/reduce_max | solution.py:44
  599.6 74.1 %pmax.15 = bf16[8192]{0:T(1024)(128)(2,1)S(1)} all-reduce(bf16[8192]{0:T(1024)(128)(2,1)S(1)} %fusion.3), channel_id=1, replica_groups=mesh['blk'=64,'grp'=4] {'blk','grp'}, use_global_device_ids=true, to_apply=%region_9.0 | all-reduce | flops 8192 | bytes 32768 | tf_op jit(solution)/shard_map/pmax | solution.py:45
  673.6 9.4 %exponential_reduce_fusion = f32[8192]{0:T(1024)S(1)} fusion(f32[512,8192]{1,0:T(8,128)} %get-tuple-element.3, f32[8192]{0:T(1024)S(1)} %convert_element_type.15, f32[512]{0:T(512)S(1)} %multiply_subtract_fusion.1), kind=kLoop, calls=%fused_computation | loop fusion | flops 16769024 | bytes 16844800 | tf_op jit(solution)/shard_map/reduce_sum | solution.py:46
  683.1 73.3 %psum.15 = f32[8192]{0:T(1024)S(1)} all-reduce(f32[8192]{0:T(1024)S(1)} %exponential_reduce_fusion), channel_id=1, replica_groups=mesh['blk'=64,'grp'=4] {'blk','grp'}, use_global_device_ids=true, to_apply=%region_11.0 | all-reduce | flops 8192 | bytes 65536 | tf_op jit(solution)/shard_map/psum | solution.py:46
  756.4 0.6 dynamic-slice_subtract_fusion
  (8 shorter events, 0.1 us)
Async XLA Ops:
  7.2 333.9 %copy-start = (bf16[512,768]{1,0:T(8,128)(2,1)S(1)}, bf16[512,768]{1,0:T(8,128)(2,1)}, u32[]{:S(2)}) copy-start(bf16[512,768]{1,0:T(8,128)(2,1)} %param.5) | copy-start | bytes 2359300
  7.2 333.8 %all-gather.3.cloned.1.call-start = ((), (), s32[]{:S(2)}) async-start(), calls=%async_computation.1 | async-start | bytes 12779520 | tf_op jit(solution)/shard_map/all_gather | solution.py:33
  9.2 175.7 %all-to-all-start = ((f32[64,1,128]{2,1,0:T(1,128)}), f32[64,1,128]{2,1,0:T(1,128)S(1)}, u32[]{:S(2)}, u32[]{:S(2)}) async-start(f32[64,1,128]{2,1,0:T(1,128)} %stack.2), calls=%async_computation | async-start | bytes 65536 | tf_op jit(solution)/shard_map/all_to_all | solution.py:25
  356.0 9.2 %copy-start.2 = (f32[512]{0:T(512)S(1)}, f32[512]{0:T(512)}, u32[]{:S(2)}) copy-start(f32[512]{0:T(512)} %param.8) | copy-start | bytes 6148
  591.2 91.9 %copy-start.1 = (f32[512]{0:T(512)}, f32[512]{0:T(512)S(1)}, u32[]{:S(2)}) copy-start(f32[512]{0:T(512)S(1)} %multiply_subtract_fusion.1) | copy-start | bytes 6148
Sparse Core Ops, SparseCore 0:
  9.8 331.2 all-gather.2

commit v2 on v0

--- a/solution.py
+++ b/solution.py
@@ -41,7 +41,10 @@
         scores = (row_pot[:, None] - cost_matrix) * inverse_eps
         col_top = jnp.max(scores, axis=0)
         col_peak = lax.pmax(col_top.astype(jnp.bfloat16), ("blk", "grp")).astype(col_top.dtype)
-        col_total = lax.psum(jnp.sum(jnp.exp(scores - col_peak[None, :]), axis=0), ("blk", "grp"))
+        col_total = jnp.sum(
+            lax.all_gather(jnp.sum(jnp.exp(scores - col_peak[None, :]), axis=0), ("blk", "grp")),
+            axis=0,
+        )
         column_pot = epsilon * logw_full - epsilon * (col_peak + jnp.log(col_total))
     return (
         row_pot,

time: 765 us -> 1480 us (1.93)
  waiting for transfers between devices: 13.2 us -> 845 us
  blocking collectives: 659 us -> 511 us
  local copies, waits for them, and re-layouts: 0.02 us -> 18.8 us
    all_gather x0 -> x2, waiting for transfers between devices: none -> 676 us  [shards(): lax.all_gather(jnp.sum(jnp.exp(scores - col_peak[None, :]), axis=0), ('bl...]
    all_gather x1, waiting for transfers between devices: 12.5 us -> 168 us  [shards(): lax.all_gather(target_embed, 'blk', axis=0, tiled=True)]
    psum x2 -> x0, blocking collectives: 146 us -> none  [shards(): lax.psum(jnp.sum(jnp.exp(scores - col_peak[None, :]), axis=0), ('blk', 'g...]
    all_gather x0 -> x2, local copies, waits for them, and re-layouts: none -> 18.8 us  [shards(): lax.all_gather(jnp.sum(jnp.exp(scores - col_peak[None, :]), axis=0), ('bl...]
  transfers between devices with their start and end apart: 1 -> 3, of which waited for: 1 -> 3; matrix products, arithmetic and copies ran while one was open for 0% -> 0% of each run, Pallas kernels for 0% -> 0%
where the time goes in v2:
time: 1480 us; the launch traced here: 1470 us
  waiting for transfers between devices  845 us (57%)
  blocking collectives  511 us (35%)
  other arithmetic  71.3 us (5%)
  local copies, waits for them, and re-layouts  18.8 us (1%)
  matrix products  14.9 us (1%)
    all_gather x2, waiting for transfers between devices, shards(): lax.all_gather(jnp.sum(jnp.exp(scores - col_peak[None, :]), axis=0), ('bl...  676 us
    pmax x2, blocking collectives, shards(): lax.pmax(col_top.astype(jnp.bfloat16), ('blk', 'grp')).astype(col_top.dtype)  194 us
    all_gather x1, waiting for transfers between devices, shards(): lax.all_gather(target_embed, 'blk', axis=0, tiled=True)  168 us
    all_gather x1, blocking collectives, shards(): lax.all_gather(target_init, 'blk', axis=0, tiled=True)  165 us
    all_gather x1, blocking collectives, shards(): lax.all_gather(target_logw, 'blk', axis=0, tiled=True)  152 us
  transfers between devices with their start and end apart: 3, of which 3 were waited for; matrix products, arithmetic and copies ran while one was open for 0% of the time, Pallas kernels for 0%

profile of v2, /device:TPU:1, one launch (start us, length us, event | category | flops | bytes accessed | tf_op | source)
XLA Modules:
  0.0 1474.8 jit_solution(18163738517826476502)
XLA Ops:
  7.2 0.0 all-gather.8.cloned.1.call-start
  7.2 0.7 all-gather.8.cloned.1.call-update
  7.9 0.0 all-gather.10.cloned.1.call-start
  8.0 164.7 %all-gather.3 = f32[64,1,128]{2,1,0:T(1,128)S(1)} all-gather(f32[1,1,128]{2,1,0:T(1,128)} %bitcast.10), channel_id=1, replica_groups=mesh['blk'=64,'grp'=4] {'blk'}, dimensions={0}, use_global_device_ids=true | all-gather | bytes 33280 | tf_op jit(solution)/shard_map/all_gather | solution.py:23
  172.7 168.3 %all-gather.8.cloned.1.call-done = bf16[8192,768]{1,0:T(8,128)(2,1)} async-done(((bf16[128,768]{1,0:T(8,128)(2,1)}), bf16[8192,768]{1,0:T(8,128)(2,1)}) %all-gather.8.cloned.1.call-update) | async-done | bytes 12582928 | tf_op jit(solution)/shard_map/all_gather | solution.py:31
  341.0 14.9 %fusion = (f32[512]{0:T(512)S(1)}, f32[512,8192]{1,0:T(8,128)}) fusion(f32[8192]{0:T(1024)S(1)} %bitcast.8, bf16[512,768]{1,0:T(8,128)(2,1)S(1)} %copy-done, bf16[8192,768]{1,0:T(8,128)(2,1)} %all-gather.8.cloned.1.call-done), kind=kOutput, calls=%fused_computation.8 | convolution fusion | flops 6459227648 | bytes 30181376 | tf_op jit(solution)/shard_map/dot_general | solution.py:29
  355.9 9.2 exponential_reduce_fusion.3
  365.1 8.4 fusion.1
  373.5 117.6 %pmax.14 = bf16[8192]{0:T(1024)(128)(2,1)S(1)} all-reduce(bf16[8192]{0:T(1024)(128)(2,1)S(1)} %fusion.1), channel_id=1, replica_groups=mesh['blk'=64,'grp'=4] {'blk','grp'}, use_global_device_ids=true, to_apply=%region_3.0 | all-reduce | flops 8192 | bytes 32768 | tf_op jit(solution)/shard_map/pmax | solution.py:43
  491.1 10.0 exponential_reduce_fusion.2
  501.1 0.0 all-gather.12.cloned.1.call-start
  501.2 152.1 %all-gather.2 = f32[64,1,128]{2,1,0:T(1,128)S(1)} all-gather(f32[1,1,128]{2,1,0:T(1,128)S(1)} %bitcast.11), channel_id=1, replica_groups=mesh['blk'=64,'grp'=4] {'blk'}, dimensions={0}, use_global_device_ids=true | all-gather | bytes 33280 | tf_op jit(solution)/shard_map/all_gather | solution.py:24
  653.3 261.8 %all-gather.10.cloned.1.call-done = f32[2097152]{0:T(1024)} async-done(((f32[8192]{0:T(1024)}), f32[2097152]{0:T(1024)}) %all-gather.10.cloned.1.call-update) | async-done | bytes 8388624 | tf_op jit(solution)/shard_map/all_gather | solution.py:45
  915.2 9.4 reshape.12
  924.5 3.8 reduce_sum.56
  928.4 7.7 fusion.2
  936.1 9.3 exponential_reduce_fusion.1
  945.5 8.4 fusion.3
  953.8 76.2 %pmax.15 = bf16[8192]{0:T(1024)(128)(2,1)S(1)} all-reduce(bf16[8192]{0:T(1024)(128)(2,1)S(1)} %fusion.3), channel_id=1, replica_groups=mesh['blk'=64,'grp'=4] {'blk','grp'}, use_global_device_ids=true, to_apply=%region_9.0 | all-reduce | flops 8192 | bytes 32768 | tf_op jit(solution)/shard_map/pmax | solution.py:43
  1030.1 10.0 exponential_reduce_fusion
  1040.1 414.4 %all-gather.12.cloned.1.call-done = f32[2097152]{0:T(1024)} async-done(((f32[8192]{0:T(1024)}), f32[2097152]{0:T(1024)}) %all-gather.12.cloned.1.call-update) | async-done | bytes 8388624 | tf_op jit(solution)/shard_map/all_gather | solution.py:45
  1454.5 9.4 reshape.13
  1463.9 3.8 reduce_sum.59
  1467.7 0.6 dynamic-slice_subtract_fusion
  (16 shorter events, 0.1 us)
Async XLA Ops:
  7.2 333.8 %copy-start = (bf16[512,768]{1,0:T(8,128)(2,1)S(1)}, bf16[512,768]{1,0:T(8,128)(2,1)}, u32[]{:S(2)}) copy-start(bf16[512,768]{1,0:T(8,128)(2,1)} %param.5) | copy-start | bytes 2359300
  7.2 333.8 %all-gather.8.cloned.1.call-start = ((), (), s32[]{:S(2)}) async-start(), calls=%async_computation | async-start | bytes 12779520 | tf_op jit(solution)/shard_map/all_gather | solution.py:31
  7.9 907.2 %all-gather.10.cloned.1.call-start = ((), (), s32[]{:S(2)}) async-start(), calls=%async_computation.1 | async-start | bytes 8421376 | tf_op jit(solution)/shard_map/all_gather | solution.py:45
  355.9 9.2 copy-start.2
  365.1 136.1 %copy-start.3 = (f32[128]{0:T(128)S(1)}, f32[128]{0:T(128)}, u32[]{:S(2)}) copy-start(f32[128]{0:T(128)} %param.9) | copy-start | bytes 1540
  501.1 953.4 %all-gather.12.cloned.1.call-start = ((), (), s32[]{:S(2)}) async-start(), calls=%async_computation.2 | async-start | bytes 8421376 | tf_op jit(solution)/shard_map/all_gather | solution.py:45
  945.5 94.6 %copy-start.1 = (f32[512]{0:T(512)}, f32[512]{0:T(512)S(1)}, u32[]{:S(2)}) copy-start(f32[512]{0:T(512)S(1)} %multiply_subtract_fusion.1) | copy-start | bytes 6148
Sparse Core Ops, SparseCore 0:
  9.8 331.1 all-gather.7
  501.2 413.8 all-gather.9
  1040.2 414.2 all-gather.11
